TPU v7x, 32 devices: a whole 2x2x4 slice. The times are simulated.
32 devices in a mesh: seq: 8 (over z, x), dp: 4 (over y, core).
Axes of the slice: x: 2, y: 2, z: 4, core: 2. Of those that a mesh axis runs over, the one named last changes fastest.
Arguments:
- bases: int32 [4, 16384], P('dp', 'seq'), may hold values from 0 to 3
- stem_table: bfloat16 [60, 256], replicated, may hold values from -1.5 to 1.5
- first_conv_taps: bfloat16 [3, 256, 128], replicated, may hold values from -0.21875 to 0.21875
- first_projection_weight: bfloat16 [128, 256], replicated, may hold values from -0.5 to 0.5
- second_conv_taps: bfloat16 [3, 256, 128], replicated, may hold values from -0.21875 to 0.21875
- second_projection_weight: bfloat16 [128, 256], replicated, may hold values from -0.5 to 0.5
- bin_weight: bfloat16 [1536, 256], P('seq'), may hold values from -0.375 to 0.375
- cotangent: bfloat16 [4, 1536, 128], P('dp', 'seq'), may hold values from -96 to 96
Outputs:
- predictions: bfloat16 [4, 1536, 128], P('dp', 'seq')
- saliency: float32 [4, 4, 16384], P('dp', None, 'seq')
- conv_one_grad: float32 [3, 256, 128], replicated
- proj_one_grad: float32 [128, 256], replicated
- conv_two_grad: float32 [3, 256, 128], replicated
- proj_two_grad: float32 [128, 256], replicated
- bin_weight_grad: float32 [1536, 256], P('seq')
All inputs are finite; a program needn't handle non-finite values.
Results may differ from a plain program's by a relative error of at most 0.015.
Values may be sent and summed in bfloat16 or wider, within the bound.
A program may use at most 64 MiB of HBM per device.

v0:
```python
import jax
import jax.numpy as jnp
from jax import lax
from jax.sharding import PartitionSpec as P

STEM = 15
POOL = 128


def passed_along(value, axis, steps):
    count = lax.axis_size(axis)
    first, last = (max(0, -steps), min(count, count - steps))
    return lax.ppermute(value, axis, [(source, source + steps) for source in range(first, last)])


def with_halo(cells, sides, width):
    for axis, dim in sides:
        count = lax.axis_size(axis)
        ends = count - 1
        head = lax.slice_in_dim(cells, 0, width, axis=dim)
        tail = lax.slice_in_dim(cells, cells.shape[dim] - width, cells.shape[dim], axis=dim)
        cells = jnp.concatenate(
            [
                lax.ppermute(tail, axis, [(i, (i + 1) % count) for i in range(ends)]),
                cells,
                lax.ppermute(head, axis, [((i + 1) % count, i) for i in range(ends)]),
            ],
            axis=dim,
        )
    return cells


def gelu_exact(value):
    return 0.5 * value * (1.0 + jax.scipy.special.erf(value * 0.7071067811865476))


def gelu_slope(value):
    return (
        0.5 * (1.0 + jax.scipy.special.erf(value * 0.7071067811865476))
        + value * jnp.exp(-0.5 * value * value) * 0.3989422804014327
    )


def tap_shift(values, hops):
    return passed_along(values, "seq", hops)


def grad_shift(values, hops):
    return passed_along(values, "seq", hops)


def reduce_grads(conv_raw, proj_raw):
    return lax.psum((conv_raw, proj_raw), ("seq", "dp"))


def residual_block_apply(stream, conv_w, proj_w, hops):
    act = gelu_exact(stream.astype(jnp.float32)).astype(jnp.bfloat16)
    before = tap_shift(act, hops)
    after = tap_shift(act, -hops)
    tap_before = jnp.dot(before, conv_w[0], preferred_element_type=jnp.float32).astype(jnp.bfloat16)
    tap_after = jnp.dot(after, conv_w[2], preferred_element_type=jnp.float32).astype(jnp.bfloat16)
    pre = jnp.dot(act, conv_w[1], preferred_element_type=jnp.float32)
    pre = pre + tap_before.astype(jnp.float32) + tap_after.astype(jnp.float32)
    inner = gelu_exact(pre).astype(jnp.bfloat16)
    result = (
        stream.astype(jnp.float32) + jnp.dot(inner, proj_w, preferred_element_type=jnp.float32)
    ).astype(jnp.bfloat16)
    return (result, (stream, act, before, after, pre, inner))


def residual_block_reverse(incoming, saved, conv_w, proj_w, hops):
    stream, act, before, after, pre, inner = saved
    grad_in = incoming.astype(jnp.bfloat16)
    inner_grad = jnp.dot(grad_in, proj_w.T, preferred_element_type=jnp.float32)
    pre_grad = (inner_grad * gelu_slope(pre)).astype(jnp.bfloat16)
    later = grad_shift(pre_grad, -hops)
    earlier = grad_shift(pre_grad, hops)
    proj_raw = jnp.dot(inner.T, grad_in, preferred_element_type=jnp.float32)
    middle = jnp.dot(act.T, pre_grad, preferred_element_type=jnp.float32)
    conv_raw = jnp.stack(
        [
            jnp.dot(before.T, pre_grad, preferred_element_type=jnp.float32),
            middle,
            jnp.dot(after.T, pre_grad, preferred_element_type=jnp.float32),
        ]
    )
    act_grad = jnp.dot(pre_grad, conv_w[1].T, preferred_element_type=jnp.float32)
    act_grad = act_grad + jnp.dot(later, conv_w[0].T, preferred_element_type=jnp.float32)
    act_grad = act_grad + jnp.dot(earlier, conv_w[2].T, preferred_element_type=jnp.float32)
    outgoing = incoming + act_grad * gelu_slope(stream.astype(jnp.float32))
    conv_sum, proj_sum = reduce_grads(conv_raw, proj_raw)
    return (outgoing, conv_sum, proj_sum)


def per_device(
    bases,
    stem_table,
    first_conv_taps,
    first_projection_weight,
    second_conv_taps,
    second_projection_weight,
    bin_weight,
    cotangent,
):
    length = bases.shape[1]
    width = stem_table.shape[1]
    half = STEM // 2
    bins_dev = length // POOL
    scale = float(lax.axis_size("dp") * lax.axis_size("seq") * length) ** (-0.5)
    padded_ids = with_halo(bases[0] + 1, (("seq", 0),), half)
    taps = jnp.stack([padded_ids[k : k + length] for k in range(STEM)], axis=1)
    letters = jnp.arange(1, 5, dtype=jnp.int32)
    codes = (
        (taps[:, :, None] == letters[None, None, :]).astype(jnp.bfloat16).reshape(length, 4 * STEM)
    )
    stem_pre = jnp.dot(codes, stem_table, preferred_element_type=jnp.float32)
    residual_input_level = gelu_exact(stem_pre).astype(jnp.bfloat16)
    residual_after_first, first_block_stash = residual_block_apply(
        residual_input_level, first_conv_taps, first_projection_weight, 1
    )
    residual_after_second, second_block_stash = residual_block_apply(
        residual_after_first, second_conv_taps, second_projection_weight, 2
    )
    pooled = jnp.mean(
        residual_after_second.astype(jnp.float32).reshape(bins_dev, POOL, width), axis=1
    )
    pooled_act = gelu_exact(pooled).astype(jnp.bfloat16)
    cot_rows = cotangent[0]
    gathered = lax.all_gather(pooled_act, "seq", axis=0, tiled=True)
    preds = lax.dot_general(
        bin_weight, gathered, (((1,), (1,)), ((), ())), preferred_element_type=jnp.float32
    ).astype(jnp.bfloat16)
    bin_part = jnp.dot(cot_rows, gathered, preferred_element_type=jnp.float32)
    summed = lax.psum_scatter(
        lax.dot_general(
            cot_rows, bin_weight, (((0,), (0,)), ((), ())), preferred_element_type=jnp.float32
        ),
        "seq",
        scatter_dimension=0,
        tiled=True,
    )
    bin_total = lax.psum(bin_part, "dp")
    pooled_grad = summed * gelu_slope(pooled)
    gradient_after_second = jnp.repeat(pooled_grad / POOL, POOL, axis=0)
    gradient_after_first, conv_two_sum, proj_two_sum = residual_block_reverse(
        gradient_after_second, second_block_stash, second_conv_taps, second_projection_weight, 2
    )
    gradient_input_level, conv_one_sum, proj_one_sum = residual_block_reverse(
        gradient_after_first, first_block_stash, first_conv_taps, first_projection_weight, 1
    )
    stem_grad = (gradient_input_level * gelu_slope(stem_pre)).astype(jnp.bfloat16)
    code_grad = jnp.dot(stem_grad, stem_table.T, preferred_element_type=jnp.float32)
    padded_grad = with_halo(code_grad.astype(jnp.bfloat16), (("seq", 0),), half).astype(
        code_grad.dtype
    )
    total = jnp.zeros((length, 4), jnp.float32)
    for k in range(STEM):
        start = 2 * half - k
        total = total + padded_grad[start : start + length, 4 * k : 4 * k + 4]
    return (
        preds[None],
        total.T[None],
        conv_one_sum * scale,
        proj_one_sum * scale,
        conv_two_sum * scale,
        proj_two_sum * scale,
        bin_total * scale,
    )


def solution(mesh):
    placed = (P("dp", "seq"), P(), P(), P(), P(), P(), P("seq", None), P("dp", "seq", None))
    return jax.shard_map(
        per_device,
        mesh=mesh,
        in_specs=placed,
        out_specs=(P("dp", "seq", None), P("dp", None, "seq"), P(), P(), P(), P(), P("seq", None)),
        check_vma=False,
    )
```

profile of v0, /device:TPU:0, one launch (start us, length us, event | category | flops | bytes accessed | tf_op | source)
XLA Modules:
  0.0 393.4 jit_solution(10875098786086386174)
XLA Ops:
  7.2 0.7 fusion.105
  8.0 1.3 collective-permute-start.1
  9.3 5.5 %collective-permute-start = (s32[7]{0:T(128)S(1)}, s32[7]{0:T(128)S(1)}, u32[]{:S(2)}, u32[]{:S(2)}) collective-permute-start(s32[7]{0:T(128)S(1)} %get-tuple-element.30), channel_id=1, source_target_pairs={{0,4},{4,8},{8,12},{12,16},{16,20},{20,24},{24,28},{1,5},{5,9},{9,... | collective-permute-start | bytes 92 | tf_op jit(solution)/shard_map/ppermute | solution.py:24
  15.0 1.1 collective-permute-done
  16.2 0.2 stack.84
  16.4 0.1 eq.20
  16.5 0.2 eq.21
  16.7 1.0 fusion.22
  17.8 4.9 %collective-permute-start.2 = (bf16[2048,256]{1,0:T(8,128)(2,1)S(1)}, bf16[2048,256]{1,0:T(8,128)(2,1)S(1)}, u32[]{:S(2)}, u32[]{:S(2)}) collective-permute-start(bf16[2048,256]{1,0:T(8,128)(2,1)S(1)} %get-tuple-element.33), channel_id=1, source_target_pairs={{0,4},{4,8},{8,12},{12,16},{16,20},{20,24},{24,28},{1,5},{5,9},{9,... | collective-permute-start | bytes 3145736 | tf_op jit(solution)/shard_map/ppermute | solution.py:13
  22.7 1.3 collective-permute-start.3
  24.0 0.4 fusion.68
  24.4 41.9 %collective-permute-done.2 = bf16[2048,256]{1,0:T(8,128)(2,1)S(1)} collective-permute-done((bf16[2048,256]{1,0:T(8,128)(2,1)S(1)}, bf16[2048,256]{1,0:T(8,128)(2,1)S(1)}, u32[]{:S(2)}, u32[]{:S(2)}) %collective-permute-start.2) | collective-permute-done | bytes 1048608 | tf_op jit(solution)/shard_map/ppermute | solution.py:13
  66.3 0.4 fusion.16
  66.8 0.4 fusion.14
  67.3 0.5 copy-done.4
  67.8 2.5 fusion.29
  70.4 6.3 %collective-permute-start.4 = (bf16[2048,256]{1,0:T(8,128)(2,1)}, bf16[2048,256]{1,0:T(8,128)(2,1)S(1)}, u32[]{:S(2)}, u32[]{:S(2)}) collective-permute-start(bf16[2048,256]{1,0:T(8,128)(2,1)} %get-tuple-element.35), channel_id=1, source_target_pairs={{0,8},{4,12},{8,16},{12,20},{16,24},{20,28},{1,9},{5,13},{9,17},{1... | collective-permute-start | bytes 3145736 | tf_op jit(solution)/shard_map/ppermute | solution.py:13
  76.6 1.3 collective-permute-start.5
  78.0 0.9 fusion.85
  78.9 1.6 fusion.59
  80.5 19.6 %collective-permute-done.4 = bf16[2048,256]{1,0:T(8,128)(2,1)S(1)} collective-permute-done((bf16[2048,256]{1,0:T(8,128)(2,1)}, bf16[2048,256]{1,0:T(8,128)(2,1)S(1)}, u32[]{:S(2)}, u32[]{:S(2)}) %collective-permute-start.4) | collective-permute-done | bytes 1048608 | tf_op jit(solution)/shard_map/ppermute | solution.py:13
  100.1 0.4 fusion.12
  100.6 3.8 collective-permute-done.5
  104.4 1.4 multiply_convert_fusion.1
  105.8 0.8 copy-done.10
  106.6 0.4 convert_reduce_fusion
  107.0 34.7 %reduce-scatter.2.cloned.1.call-done = f32[16,256]{1,0:T(8,128)} async-done(((f32[128,256]{1,0:T(8,128)}), f32[16,256]{1,0:T(8,128)}) %reduce-scatter.2.cloned.1.call-update) | async-done | bytes 16400 | tf_op jit(solution)/shard_map/reduce_scatter | solution.py:134
  141.7 0.8 multiply_multiply_fusion.3
  142.5 2.0 fusion.107
  144.6 1.4 fusion.7
  146.0 2.5 convolution_bitcast_fusion.2
  148.4 1.5 fusion.57
  149.9 1.3 collective-permute-start.6
  151.2 5.4 %collective-permute-start.7 = (bf16[2048,128]{1,0:T(8,128)(2,1)}, bf16[2048,128]{1,0:T(8,128)(2,1)}, u32[]{:S(2)}, u32[]{:S(2)}) collective-permute-start(bf16[2048,128]{1,0:T(8,128)(2,1)} %fusion.7), channel_id=1, source_target_pairs={{0,8},{4,12},{8,16},{12,20},{16,24},{20,28},{1,9},{5,13},{9,17},{1... | collective-permute-start | bytes 1572872 | tf_op jit(solution)/shard_map/ppermute | solution.py:13
  156.6 33.8 %all_gather.3 = bf16[128,256]{1,0:T(8,128)(2,1)S(1)} all-gather(bf16[16,256]{1,0:T(8,128)(2,1)S(1)} %get-tuple-element.14), channel_id=1, replica_groups=mesh['seq'=8,'dp'=4] {'seq'}, dimensions={0}, use_global_device_ids=true | all-gather | bytes 73728 | tf_op jit(solution)/shard_map/all_gather | solution.py:129
  190.4 0.8 convolution_bitcast_fusion
  191.2 0.8 fusion.35
  192.1 1.9 convolution_bitcast_fusion.1
  194.0 1.8 convolution_bitcast_fusion.3
  195.8 0.8 pad_maximum_fusion.1
  196.6 1.6 convolution_add_fusion.3
  198.2 2.2 bitcast_add_fusion
  200.5 1.1 fusion.47
  201.5 2.0 fusion.8
  203.5 0.5 convolution_bitcast_fusion.5
  204.0 0.5 convolution_bitcast_fusion.4
  204.5 0.2 copy-done.3
  204.7 0.5 convolution_bitcast_fusion.6
  205.2 0.8 pad_maximum_fusion
  206.0 18.0 %all-reduce.4.cloned.1.call-done = f32[192,256]{1,0:T(8,128)} async-done(((f32[192,256]{1,0:T(8,128)}), f32[192,256]{1,0:T(8,128)}) %all-reduce.4.cloned.1.call-update) | async-done | bytes 196624 | tf_op jit(solution)/shard_map/psum | solution.py:142
  224.0 1.6 broadcast_multiply_fusion.2
  225.6 1.3 collective-permute-start.8
  226.9 5.4 %collective-permute-start.9 = (bf16[2048,128]{1,0:T(8,128)(2,1)S(1)}, bf16[2048,128]{1,0:T(8,128)(2,1)}, u32[]{:S(2)}, u32[]{:S(2)}) collective-permute-start(bf16[2048,128]{1,0:T(8,128)(2,1)S(1)} %fusion.8), channel_id=1, source_target_pairs={{0,4},{4,8},{8,12},{12,16},{16,20},{20,24},{24,28},{1,5},{5,9},{9,... | collective-permute-start | bytes 1572872 | tf_op jit(solution)/shard_map/ppermute | solution.py:13
  232.3 1.8 fusion.66
  234.1 132.3 %all-reduce.6.cloned.1.call-done = (f32[3,256,128]{2,1,0:T(8,128)}, f32[128,256]{1,0:T(8,128)}, f32[3,256,128]{2,1,0:T(8,128)}, f32[128,256]{1,0:T(8,128)}) async-done(((f32[3,256,128]{2,1,0:T(8,128)}, f32[128,256]{1,0:T(8,128)}, f32[3,256,128]{2,1,0:T(8,128)}, f32[128,256]{1,0:T(8,128)}), (f32[3,256,128]{2,1,0:T(8,128)}, f32[128,256]{1,0:T(8,128)}, f32[3,256,128]{2,1,0:T(8,128)}, ...) | async-done | bytes 1048592 | tf_op jit(solution)/shard_map/psum | solution.py:53
  366.3 2.0 broadcast_multiply_fusion
  368.4 3.5 convolution_add_fusion.1
  371.9 4.6 %convolution_convert_fusion.4 = bf16[2048,60]{0,1:T(8,128)(2,1)S(1)} fusion(bf16[60,256]{1,0:T(8,128)(2,1)S(1)} %copy-done.28, f32[2048,256]{1,0:T(8,128)S(1)} %bitcast_add_fusion, f32[2048,256]{1,0:T(8,128)} %convolution_add_fusion.1, bf16[2048,128]{1,0:T(8,128)(2,1)} %collective-permute-done.9, f32[2048,256]{1,0:T(8,128)} %copy-done.29, ...), kind=kOutput, calls=%fused_computation.42 | convolution fusion | flops 210362368 | bytes 7159808 | tf_op jit(solution)/shard_map/dot_general | solution.py:152
  376.6 3.4 collective-permute-start.10
  380.0 1.3 collective-permute-start.11
  381.3 0.7 broadcast_multiply_fusion.3
  382.0 3.6 collective-permute-done.11
  385.6 0.3 concatenate.24
  385.9 0.9 fusion.87
  (79 shorter events, 0.9 us)
Async XLA Ops:
  7.2 70.8 %copy-start = (bf16[192,256]{1,0:T(8,128)(2,1)S(1)}, bf16[192,256]{1,0:T(8,128)(2,1)}, u32[]{:S(2)}) copy-start(bf16[192,256]{1,0:T(8,128)(2,1)} %param.14) | copy-start | bytes 294916
  7.2 9.5 %copy-start.27 = (bf16[60,256]{1,0:T(8,128)(2,1)S(1)}, bf16[60,256]{1,0:T(8,128)(2,1)}, u32[]{:S(2)}) copy-start(bf16[60,256]{1,0:T(8,128)(2,1)} %param.9) | copy-start | bytes 92164
  7.2 134.5 %reduce-scatter.2.cloned.1.call-start = ((), (), s32[]{:S(2)}) async-start(), calls=%async_computation.1 | async-start | bytes 147456 | tf_op jit(solution)/shard_map/reduce_scatter | solution.py:134
  8.0 6.9 %collective-permute-start.1 = (s32[7]{0:T(128)S(1)}, s32[7]{0:T(128)S(1)}, u32[]{:S(2)}, u32[]{:S(2)}) collective-permute-start(s32[7]{0:T(128)S(1)} %get-tuple-element.29), channel_id=1, source_target_pairs={{4,0},{8,4},{12,8},{16,12},{20,16},{24,20},{28,24},{5,1},{9,5},{13... | collective-permute-start | bytes 92 | tf_op jit(solution)/shard_map/ppermute | solution.py:26
  9.3 6.8 %collective-permute-start = (s32[7]{0:T(128)S(1)}, s32[7]{0:T(128)S(1)}, u32[]{:S(2)}, u32[]{:S(2)}) collective-permute-start(s32[7]{0:T(128)S(1)} %get-tuple-element.30), channel_id=1, source_target_pairs={{0,4},{4,8},{8,12},{12,16},{16,20},{20,24},{24,28},{1,5},{5,9},{9,... | collective-permute-start | bytes 92 | tf_op jit(solution)/shard_map/ppermute | solution.py:24
  16.7 7.3 %copy-start.15 = (bf16[3,256,128]{2,1,0:T(8,128)(2,1)S(1)}, bf16[3,256,128]{2,1,0:T(8,128)(2,1)}, u32[]{:S(2)}) copy-start(bf16[3,256,128]{2,1,0:T(8,128)(2,1)} %param.10) | copy-start | bytes 589828
  17.7 49.0 %copy-start.8 = (bf16[2048,256]{1,0:T(8,128)(2,1)}, bf16[2048,256]{1,0:T(8,128)(2,1)S(1)}, u32[]{:S(2)}) copy-start(bf16[2048,256]{1,0:T(8,128)(2,1)S(1)} %get-tuple-element.33) | copy-start | bytes 3145732
  17.8 50.0 %copy-start.29 = (f32[2048,256]{1,0:T(8,128)}, f32[2048,256]{1,0:T(8,128)S(1)}, u32[]{:S(2)}) copy-start(f32[2048,256]{1,0:T(8,128)S(1)} %get-tuple-element.34) | copy-start | bytes 6291460
  17.8 48.6 %collective-permute-start.2 = (bf16[2048,256]{1,0:T(8,128)(2,1)S(1)}, bf16[2048,256]{1,0:T(8,128)(2,1)S(1)}, u32[]{:S(2)}, u32[]{:S(2)}) collective-permute-start(bf16[2048,256]{1,0:T(8,128)(2,1)S(1)} %get-tuple-element.33), channel_id=1, source_target_pairs={{0,4},{4,8},{8,12},{12,16},{16,20},{20,24},{24,28},{1,5},{5,9},{9,... | collective-permute-start | bytes 3145736 | tf_op jit(solution)/shard_map/ppermute | solution.py:13
  22.7 44.1 %collective-permute-start.3 = (bf16[2048,256]{1,0:T(8,128)(2,1)S(1)}, bf16[2048,256]{1,0:T(8,128)(2,1)S(1)}, u32[]{:S(2)}, u32[]{:S(2)}) collective-permute-start(bf16[2048,256]{1,0:T(8,128)(2,1)S(1)} %get-tuple-element.33), channel_id=1, source_target_pairs={{4,0},{8,4},{12,8},{16,12},{20,16},{24,20},{28,24},{5,1},{9,5},{13... | collective-permute-start | bytes 3145736 | tf_op jit(solution)/shard_map/ppermute | solution.py:13
  66.3 1.0 copy-start.2
  66.8 1.0 copy-start.23
  66.8 1.0 copy-start.4
  67.8 132.6 %copy-start.1 = (f32[2048,128]{1,0:T(8,128)}, f32[2048,128]{1,0:T(8,128)S(1)}, u32[]{:S(2)}) copy-start(f32[2048,128]{1,0:T(8,128)S(1)} %fusion.14) | copy-start | bytes 3145732
  67.8 10.2 %copy-start.18 = (bf16[1,192,128]{2,1,0:T(8,128)(2,1)S(1)}, bf16[1,192,128]{2,1,0:T(8,128)(2,1)}, u32[]{:S(2)}) copy-start(bf16[1,192,128]{2,1,0:T(8,128)(2,1)} %param.15) | copy-start | bytes 147460
  67.8 11.1 %copy-start.14 = (bf16[3,256,128]{2,1,0:T(8,128)(2,1)S(1)}, bf16[3,256,128]{2,1,0:T(8,128)(2,1)}, u32[]{:S(2)}) copy-start(bf16[3,256,128]{2,1,0:T(8,128)(2,1)} %param.12) | copy-start | bytes 589828
  70.4 29.8 %collective-permute-start.4 = (bf16[2048,256]{1,0:T(8,128)(2,1)}, bf16[2048,256]{1,0:T(8,128)(2,1)S(1)}, u32[]{:S(2)}, u32[]{:S(2)}) collective-permute-start(bf16[2048,256]{1,0:T(8,128)(2,1)} %get-tuple-element.35), channel_id=1, source_target_pairs={{0,8},{4,12},{8,16},{12,20},{16,24},{20,28},{1,9},{5,13},{9,17},{1... | collective-permute-start | bytes 3145736 | tf_op jit(solution)/shard_map/ppermute | solution.py:13
  76.6 27.7 %collective-permute-start.5 = (bf16[2048,256]{1,0:T(8,128)(2,1)}, bf16[2048,256]{1,0:T(8,128)(2,1)S(1)}, u32[]{:S(2)}, u32[]{:S(2)}) collective-permute-start(bf16[2048,256]{1,0:T(8,128)(2,1)} %get-tuple-element.35), channel_id=1, source_target_pairs={{8,0},{12,4},{16,8},{20,12},{24,16},{28,20},{9,1},{13,5},{17,9},{2... | collective-permute-start | bytes 3145736 | tf_op jit(solution)/shard_map/ppermute | solution.py:13
  78.8 145.2 %all-reduce.4.cloned.1.call-start = ((), (), s32[]{:S(2)}) async-start(), calls=%async_computation.2 | async-start | bytes 393216 | tf_op jit(solution)/shard_map/psum | solution.py:142
  100.1 5.6 %copy-start.6 = (bf16[2048,256]{1,0:T(8,128)(2,1)}, bf16[2048,256]{1,0:T(8,128)(2,1)S(1)}, u32[]{:S(2)}) copy-start(bf16[2048,256]{1,0:T(8,128)(2,1)S(1)} %collective-permute-done.4) | copy-start | bytes 3145732
  100.6 6.0 %copy-start.12 = (bf16[2048,256]{1,0:T(8,128)(2,1)S(1)}, bf16[2048,256]{1,0:T(8,128)(2,1)}, u32[]{:S(2)}) copy-start(bf16[2048,256]{1,0:T(8,128)(2,1)} %get-tuple-element.36) | copy-start | bytes 3145732
  100.6 6.0 %copy-start.25 = (bf16[128,256]{1,0:T(8,128)(2,1)S(1)}, bf16[128,256]{1,0:T(8,128)(2,1)}, u32[]{:S(2)}) copy-start(bf16[128,256]{1,0:T(8,128)(2,1)} %param.13) | copy-start | bytes 196612
  104.4 2.6 copy-start.7
  105.8 0.8 copy-start.10
  106.6 38.0 %copy-start.11 = (f32[2048,128]{1,0:T(8,128)S(1)}, f32[2048,128]{1,0:T(8,128)}, u32[]{:S(2)}) copy-start(f32[2048,128]{1,0:T(8,128)} %get-tuple-element.38) | copy-start | bytes 3145732
  141.7 2.9 copy-start.26
  142.4 3.5 copy-start.19
  149.9 46.7 %collective-permute-start.6 = (bf16[2048,128]{1,0:T(8,128)(2,1)}, bf16[2048,128]{1,0:T(8,128)(2,1)}, u32[]{:S(2)}, u32[]{:S(2)}) collective-permute-start(bf16[2048,128]{1,0:T(8,128)(2,1)} %fusion.7), channel_id=1, source_target_pairs={{8,0},{12,4},{16,8},{20,12},{24,16},{28,20},{9,1},{13,5},{17,9},{2... | collective-permute-start | bytes 1572872 | tf_op jit(solution)/shard_map/ppermute | solution.py:13
  151.2 47.0 %collective-permute-start.7 = (bf16[2048,128]{1,0:T(8,128)(2,1)}, bf16[2048,128]{1,0:T(8,128)(2,1)}, u32[]{:S(2)}, u32[]{:S(2)}) collective-permute-start(bf16[2048,128]{1,0:T(8,128)(2,1)} %fusion.7), channel_id=1, source_target_pairs={{0,8},{4,12},{8,16},{12,20},{16,24},{20,28},{1,9},{5,13},{9,17},{1... | collective-permute-start | bytes 1572872 | tf_op jit(solution)/shard_map/ppermute | solution.py:13
  192.0 174.3 %all-reduce.6.cloned.1.call-start = ((), (), s32[]{:S(2)}) async-start(), calls=%async_computation.3 | async-start | bytes 2097152 | tf_op jit(solution)/shard_map/psum | solution.py:53
  192.1 3.7 copy-start.17
  196.6 1.6 copy-start.13
  196.6 1.6 copy-start.20
  200.4 1.1 copy-start.24
  201.5 2.0 copy-start.9
  201.5 2.5 copy-start.5
  203.5 1.2 copy-start.3
  204.7 27.5 %copy-start.16 = (bf16[3,256,128]{2,1,0:T(8,128)(2,1)S(1)}, bf16[3,256,128]{2,1,0:T(8,128)(2,1)}, u32[]{:S(2)}) copy-start(bf16[3,256,128]{2,1,0:T(8,128)(2,1)} %param.10) | copy-start | bytes 589828
  225.6 142.7 %collective-permute-start.8 = (bf16[2048,128]{1,0:T(8,128)(2,1)S(1)}, bf16[2048,128]{1,0:T(8,128)(2,1)}, u32[]{:S(2)}, u32[]{:S(2)}) collective-permute-start(bf16[2048,128]{1,0:T(8,128)(2,1)S(1)} %fusion.8), channel_id=1, source_target_pairs={{4,0},{8,4},{12,8},{16,12},{20,16},{24,20},{28,24},{5,1},{9,5},{13... | collective-permute-start | bytes 1572872 | tf_op jit(solution)/shard_map/ppermute | solution.py:13
  226.9 145.0 %collective-permute-start.9 = (bf16[2048,128]{1,0:T(8,128)(2,1)S(1)}, bf16[2048,128]{1,0:T(8,128)(2,1)}, u32[]{:S(2)}, u32[]{:S(2)}) collective-permute-start(bf16[2048,128]{1,0:T(8,128)(2,1)S(1)} %fusion.8), channel_id=1, source_target_pairs={{0,4},{4,8},{8,12},{12,16},{16,20},{20,24},{24,28},{1,5},{5,9},{9,... | collective-permute-start | bytes 1572872 | tf_op jit(solution)/shard_map/ppermute | solution.py:13
  368.3 3.6 copy-start.28
  371.9 9.4 %copy-start.21 = (f32[128,256]{1,0:T(8,128)S(1)}, f32[128,256]{1,0:T(8,128)}, u32[]{:S(2)}) copy-start(f32[128,256]{1,0:T(8,128)} %get-tuple-element.8) | copy-start | bytes 393220
  371.9 9.4 %copy-start.22 = (f32[128,256]{1,0:T(8,128)S(1)}, f32[128,256]{1,0:T(8,128)}, u32[]{:S(2)}) copy-start(f32[128,256]{1,0:T(8,128)} %get-tuple-element.10) | copy-start | bytes 393220
  376.6 5.4 %collective-permute-start.10 = (bf16[7,60]{0,1:T(8,128)(2,1)S(1)}, bf16[7,60]{0,1:T(8,128)(2,1)S(1)}, u32[]{:S(2)}, u32[]{:S(2)}) collective-permute-start(bf16[7,60]{0,1:T(8,128)(2,1)S(1)} %get-tuple-element.12), channel_id=1, source_target_pairs={{0,4},{4,8},{8,12},{12,16},{16,20},{20,24},{24,28},{1,5},{5,9},{9,... | collective-permute-start | bytes 2528 | tf_op jit(solution)/shard_map/ppermute | solution.py:24
  380.0 5.6 %collective-permute-start.11 = (bf16[7,60]{0,1:T(8,128)(2,1)S(1)}, bf16[7,60]{0,1:T(8,128)(2,1)S(1)}, u32[]{:S(2)}, u32[]{:S(2)}) collective-permute-start(bf16[7,60]{0,1:T(8,128)(2,1)S(1)} %get-tuple-element.11), channel_id=1, source_target_pairs={{4,0},{8,4},{12,8},{16,12},{20,16},{24,20},{28,24},{5,1},{9,5},{13... | collective-permute-start | bytes 2528 | tf_op jit(solution)/shard_map/ppermute | solution.py:26
Sparse Core Ops, SparseCore 0:
  79.0 62.6 reduce-scatter.1
  192.2 31.8 all-reduce.3
  231.1 135.1 all-reduce.5
where the time goes:
time: 394 us; the launch traced here: 393 us
  waiting for transfers between devices  255 us (65%)
  matrix products  40.4 us (10%)
  starting transfers between devices  38.6 us (10%)
  blocking collectives  33.8 us (9%)
  between operations  14.3 us (4%)
  other arithmetic  8.53 us (2%)
    psum x1, waiting for transfers between devices, reduce_grads(): return lax.psum((conv_raw, proj_raw), ('seq', 'dp'))  132 us
    ppermute x8, waiting for transfers between devices, passed_along(): lax.ppermute(value, axis, [(source, source + steps) for source in range(f...  65.3 us
    reduce_scatter x1, waiting for transfers between devices, per_device(): lax.psum_scatter(lax.dot_general(cot_rows, bin_weight, (((0,), (0,)), (()...  34.7 us
    all_gather x1, blocking collectives, per_device(): gathered = lax.all_gather(pooled_act, 'seq', axis=0, tiled=True)  33.8 us
    ppermute x8, starting transfers between devices, passed_along(): lax.ppermute(value, axis, [(source, source + steps) for source in range(f...  27 us
    psum x1, waiting for transfers between devices, per_device(): bin_total = lax.psum(bin_part, 'dp')  18 us
    ppermute x2, starting transfers between devices, with_halo(): lax.ppermute(tail, axis, [(i, (i + 1) % count) for i in range(ends)])  8.85 us
  transfers between devices with their start and end apart: 15, of which 8 were waited for; matrix products, arithmetic and copies ran while one was open for 8% of the time, Pallas kernels for 0%

commit v1 on v0

--- a/solution.py
+++ b/solution.py
@@ -50,7 +50,7 @@
 
 
 def reduce_grads(conv_raw, proj_raw):
-    return lax.psum((conv_raw, proj_raw), ("seq", "dp"))
+    return lax.psum(lax.psum((conv_raw, proj_raw), "dp"), "seq")
 
 
 def residual_block_apply(stream, conv_w, proj_w, hops):

time: 394 us -> 332 us (0.84)
  waiting for transfers between devices: 255 us -> 208 us
  matrix products: 40.4 us -> 26.3 us
    psum x2, waiting for transfers between devices: 150 us -> 102 us  [reduce_grads(): return lax.psum(lax.psum((conv_raw, proj_raw), 'dp'), 'seq')]
  transfers between devices with their start and end apart: 15 -> 15, of which waited for: 8 -> 9; matrix products, arithmetic and copies ran while one was open for 8% -> 6% of each run, Pallas kernels for 0% -> 0%
where the time goes in v1:
time: 332 us; the launch traced here: 331 us
  waiting for transfers between devices  208 us (63%)
  starting transfers between devices  37.9 us (11%)
  blocking collectives  31.9 us (10%)
  matrix products  26.3 us (8%)
  between operations  14.3 us (4%)
  other arithmetic  8.66 us (3%)
  local copies, waits for them, and re-layouts  3.91 us (1%)
    psum x2, waiting for transfers between devices, reduce_grads(): return lax.psum(lax.psum((conv_raw, proj_raw), 'dp'), 'seq')  102 us
    ppermute x8, waiting for transfers between devices, passed_along(): lax.ppermute(value, axis, [(source, source + steps) for source in range(f...  67.4 us
    reduce_scatter x1, waiting for transfers between devices, per_device(): lax.psum_scatter(lax.dot_general(cot_rows, bin_weight, (((0,), (0,)), (()...  34.2 us
    all_gather x1, blocking collectives, per_device(): gathered = lax.all_gather(pooled_act, 'seq', axis=0, tiled=True)  31.9 us
    ppermute x8, starting transfers between devices, passed_along(): lax.ppermute(value, axis, [(source, source + steps) for source in range(f...  26.3 us
    ppermute x2, starting transfers between devices, with_halo(): lax.ppermute(tail, axis, [(i, (i + 1) % count) for i in range(ends)])  8.96 us
  transfers between devices with their start and end apart: 15, of which 9 were waited for; matrix products, arithmetic and copies ran while one was open for 6% of the time, Pallas kernels for 0%

profile of v1, /device:TPU:0, one launch (start us, length us, event | category | flops | bytes accessed | tf_op | source)
XLA Modules:
  0.0 331.0 jit_solution(8971818017138685575)
XLA Ops:
  7.2 0.7 fusion.105
  8.0 1.3 collective-permute-start.1
  9.3 5.5 %collective-permute-start = (s32[7]{0:T(128)S(1)}, s32[7]{0:T(128)S(1)}, u32[]{:S(2)}, u32[]{:S(2)}) collective-permute-start(s32[7]{0:T(128)S(1)} %get-tuple-element.35), channel_id=1, source_target_pairs={{0,4},{4,8},{8,12},{12,16},{16,20},{20,24},{24,28},{1,5},{5,9},{9,... | collective-permute-start | bytes 92 | tf_op jit(solution)/shard_map/ppermute | solution.py:24
  15.0 1.1 collective-permute-done
  16.2 0.2 stack.84
  16.7 1.0 fusion.22
  17.8 4.9 %collective-permute-start.2 = (bf16[2048,256]{1,0:T(8,128)(2,1)S(1)}, bf16[2048,256]{1,0:T(8,128)(2,1)S(1)}, u32[]{:S(2)}, u32[]{:S(2)}) collective-permute-start(bf16[2048,256]{1,0:T(8,128)(2,1)S(1)} %get-tuple-element.38), channel_id=1, source_target_pairs={{0,4},{4,8},{8,12},{12,16},{16,20},{20,24},{24,28},{1,5},{5,9},{9,... | collective-permute-start | bytes 3145736 | tf_op jit(solution)/shard_map/ppermute | solution.py:13
  22.7 1.3 collective-permute-start.3
  24.0 0.4 fusion.68
  24.4 41.9 %collective-permute-done.2 = bf16[2048,256]{1,0:T(8,128)(2,1)S(1)} collective-permute-done((bf16[2048,256]{1,0:T(8,128)(2,1)S(1)}, bf16[2048,256]{1,0:T(8,128)(2,1)S(1)}, u32[]{:S(2)}, u32[]{:S(2)}) %collective-permute-start.2) | collective-permute-done | bytes 1048608 | tf_op jit(solution)/shard_map/ppermute | solution.py:13
  66.3 0.4 fusion.16
  66.8 0.4 fusion.14
  67.3 0.5 copy-done.5
  67.8 2.3 fusion.29
  70.1 6.3 %collective-permute-start.4 = (bf16[2048,256]{1,0:T(8,128)(2,1)S(1)}, bf16[2048,256]{1,0:T(8,128)(2,1)S(1)}, u32[]{:S(2)}, u32[]{:S(2)}) collective-permute-start(bf16[2048,256]{1,0:T(8,128)(2,1)S(1)} %get-tuple-element.40), channel_id=1, source_target_pairs={{0,8},{4,12},{8,16},{12,20},{16,24},{20,28},{1,9},{5,13},{9,17},{1... | collective-permute-start | bytes 3145736 | tf_op jit(solution)/shard_map/ppermute | solution.py:13
  76.4 1.3 collective-permute-start.5
  77.7 0.9 fusion.85
  78.6 0.4 fusion.59
  79.0 20.5 %collective-permute-done.4 = bf16[2048,256]{1,0:T(8,128)(2,1)S(1)} collective-permute-done((bf16[2048,256]{1,0:T(8,128)(2,1)S(1)}, bf16[2048,256]{1,0:T(8,128)(2,1)S(1)}, u32[]{:S(2)}, u32[]{:S(2)}) %collective-permute-start.4) | collective-permute-done | bytes 1048608 | tf_op jit(solution)/shard_map/ppermute | solution.py:13
  99.5 0.4 fusion.12
  100.0 3.9 %collective-permute-done.5 = bf16[2048,256]{1,0:T(8,128)(2,1)S(1)} collective-permute-done((bf16[2048,256]{1,0:T(8,128)(2,1)S(1)}, bf16[2048,256]{1,0:T(8,128)(2,1)S(1)}, u32[]{:S(2)}, u32[]{:S(2)}) %collective-permute-start.5) | collective-permute-done | bytes 1048608 | tf_op jit(solution)/shard_map/ppermute | solution.py:13
  103.9 1.5 multiply_convert_fusion.1
  105.3 0.8 copy-done.9
  106.2 1.0 convert_reduce_fusion
  107.2 34.2 %reduce-scatter.2.cloned.1.call-done = f32[16,256]{1,0:T(8,128)} async-done(((f32[128,256]{1,0:T(8,128)}), f32[16,256]{1,0:T(8,128)}) %reduce-scatter.2.cloned.1.call-update) | async-done | bytes 16400 | tf_op jit(solution)/shard_map/reduce_scatter | solution.py:134
  141.4 0.8 multiply_multiply_fusion.3
  142.3 2.0 fusion.107
  144.4 0.6 fusion.7
  145.0 0.5 convolution_bitcast_fusion.2
  145.4 1.3 collective-permute-start.6
  146.7 4.6 %collective-permute-start.7 = (bf16[2048,128]{1,0:T(8,128)(2,1)S(1)}, bf16[2048,128]{1,0:T(8,128)(2,1)S(1)}, u32[]{:S(2)}, u32[]{:S(2)}) collective-permute-start(bf16[2048,128]{1,0:T(8,128)(2,1)S(1)} %fusion.7), channel_id=1, source_target_pairs={{0,8},{4,12},{8,16},{12,20},{16,24},{20,28},{1,9},{5,13},{9,17},{1... | collective-permute-start | bytes 1572872 | tf_op jit(solution)/shard_map/ppermute | solution.py:13
  151.3 0.5 convolution_bitcast_fusion.1
  151.8 0.5 convolution_bitcast_fusion.3
  152.3 0.8 pad_maximum_fusion.1
  153.1 31.9 %all_gather.3 = bf16[128,256]{1,0:T(8,128)(2,1)S(1)} all-gather(bf16[16,256]{1,0:T(8,128)(2,1)S(1)} %get-tuple-element.19), channel_id=1, replica_groups=mesh['seq'=8,'dp'=4] {'seq'}, dimensions={0}, use_global_device_ids=true | all-gather | bytes 73728 | tf_op jit(solution)/shard_map/all_gather | solution.py:129
  184.9 0.4 fusion.57
  185.4 0.8 convolution_bitcast_fusion
  186.2 0.4 convolution_add_fusion.3
  186.7 0.8 copy-done.12
  187.4 1.1 bitcast_add_fusion
  188.6 0.6 fusion.8
  189.2 0.6 copy-done.8
  189.8 0.5 convolution_bitcast_fusion.5
  190.2 1.3 collective-permute-start.8
  191.6 5.4 %collective-permute-start.9 = (bf16[2048,128]{1,0:T(8,128)(2,1)S(1)}, bf16[2048,128]{1,0:T(8,128)(2,1)}, u32[]{:S(2)}, u32[]{:S(2)}) collective-permute-start(bf16[2048,128]{1,0:T(8,128)(2,1)S(1)} %fusion.8), channel_id=1, source_target_pairs={{0,4},{4,8},{8,12},{12,16},{16,20},{20,24},{24,28},{1,5},{5,9},{9,... | collective-permute-start | bytes 1572872 | tf_op jit(solution)/shard_map/ppermute | solution.py:13
  196.9 0.5 convolution_bitcast_fusion.4
  197.4 0.5 convolution_bitcast_fusion.6
  197.9 0.8 pad_maximum_fusion
  198.7 1.1 fusion.47
  199.8 0.4 fusion.66
  200.3 1.1 collective-permute-done.8
  201.3 1.8 convolution_add_fusion.1
  203.1 34.2 %all-reduce.7.cloned.1.call-done = (f32[3,256,128]{2,1,0:T(8,128)}, f32[128,256]{1,0:T(8,128)}, f32[3,256,128]{2,1,0:T(8,128)}, f32[128,256]{1,0:T(8,128)}, f32[192,256]{1,0:T(8,128)}) async-done(((f32[3,256,128]{2,1,0:T(8,128)}, f32[128,256]{1,0:T(8,128)}, f32[3,256,128]{2,1,0:T(8,128)}, f32[128,256]{1,0:T(8,128)}, f32[192,256]{1,0:T(8,128)}), (f32[3,256,128]{2,1,0:T(8,128)}, f32[128,256]{1,0:T(8,128)}, ...) | async-done | bytes 1245200 | tf_op jit(solution)/shard_map/psum | solution.py:53
  237.4 4.6 %convolution_convert_fusion.4 = bf16[2048,60]{0,1:T(8,128)(2,1)S(1)} fusion(bf16[60,256]{1,0:T(8,128)(2,1)S(1)} %copy-done.22, f32[2048,256]{1,0:T(8,128)S(1)} %bitcast_add_fusion, f32[2048,256]{1,0:T(8,128)} %convolution_add_fusion.1, bf16[2048,128]{1,0:T(8,128)(2,1)} %collective-permute-done.9, f32[2048,256]{1,0:T(8,128)} %copy-done.23, ...), kind=kOutput, calls=%fused_computation.42 | convolution fusion | flops 210362368 | bytes 7159808 | tf_op jit(solution)/shard_map/dot_general | solution.py:152
  242.0 3.5 %collective-permute-start.10 = (bf16[7,60]{0,1:T(8,128)(2,1)S(1)}, bf16[7,60]{0,1:T(8,128)(2,1)S(1)}, u32[]{:S(2)}, u32[]{:S(2)}) collective-permute-start(bf16[7,60]{0,1:T(8,128)(2,1)S(1)} %get-tuple-element.17), channel_id=1, source_target_pairs={{0,4},{4,8},{8,12},{12,16},{16,20},{20,24},{24,28},{1,5},{5,9},{9,... | collective-permute-start | bytes 2528 | tf_op jit(solution)/shard_map/ppermute | solution.py:24
  245.5 1.3 collective-permute-start.11
  246.8 0.8 fusion.35
  247.7 3.8 %collective-permute-done.11 = bf16[7,60]{0,1:T(8,128)(2,1)S(1)} collective-permute-done((bf16[7,60]{0,1:T(8,128)(2,1)S(1)}, bf16[7,60]{0,1:T(8,128)(2,1)S(1)}, u32[]{:S(2)}, u32[]{:S(2)}) %collective-permute-start.11) | collective-permute-done | bytes 872 | tf_op jit(solution)/shard_map/ppermute | solution.py:26
  251.5 0.3 concatenate.24
  251.8 0.9 fusion.87
  252.7 0.7 broadcast_multiply_fusion.2
  253.4 67.3 %all-reduce.5.cloned.1.call-done = (f32[3,256,128]{2,1,0:T(8,128)}, f32[128,256]{1,0:T(8,128)}, f32[3,256,128]{2,1,0:T(8,128)}, f32[128,256]{1,0:T(8,128)}) async-done(((f32[3,256,128]{2,1,0:T(8,128)}, f32[128,256]{1,0:T(8,128)}, f32[3,256,128]{2,1,0:T(8,128)}, f32[128,256]{1,0:T(8,128)}), (f32[3,256,128]{2,1,0:T(8,128)}, f32[128,256]{1,0:T(8,128)}, f32[3,256,128]{2,1,0:T(8,128)}, ...) | async-done | bytes 1048592 | tf_op jit(solution)/shard_map/psum | solution.py:53
  320.7 1.7 broadcast_multiply_fusion.3
  322.4 2.0 broadcast_multiply_fusion
  (67 shorter events, 1.2 us)
Async XLA Ops:
  7.2 70.5 %copy-start = (bf16[192,256]{1,0:T(8,128)(2,1)S(1)}, bf16[192,256]{1,0:T(8,128)(2,1)}, u32[]{:S(2)}) copy-start(bf16[192,256]{1,0:T(8,128)(2,1)} %param.14) | copy-start | bytes 294916
  7.2 9.5 %copy-start.21 = (bf16[60,256]{1,0:T(8,128)(2,1)S(1)}, bf16[60,256]{1,0:T(8,128)(2,1)}, u32[]{:S(2)}) copy-start(bf16[60,256]{1,0:T(8,128)(2,1)} %param.9) | copy-start | bytes 92164
  7.2 134.2 %reduce-scatter.2.cloned.1.call-start = ((), (), s32[]{:S(2)}) async-start(), calls=%async_computation.1 | async-start | bytes 147456 | tf_op jit(solution)/shard_map/reduce_scatter | solution.py:134
  8.0 6.9 %collective-permute-start.1 = (s32[7]{0:T(128)S(1)}, s32[7]{0:T(128)S(1)}, u32[]{:S(2)}, u32[]{:S(2)}) collective-permute-start(s32[7]{0:T(128)S(1)} %get-tuple-element.34), channel_id=1, source_target_pairs={{4,0},{8,4},{12,8},{16,12},{20,16},{24,20},{28,24},{5,1},{9,5},{13... | collective-permute-start | bytes 92 | tf_op jit(solution)/shard_map/ppermute | solution.py:26
  9.3 6.8 %collective-permute-start = (s32[7]{0:T(128)S(1)}, s32[7]{0:T(128)S(1)}, u32[]{:S(2)}, u32[]{:S(2)}) collective-permute-start(s32[7]{0:T(128)S(1)} %get-tuple-element.35), channel_id=1, source_target_pairs={{0,4},{4,8},{8,12},{12,16},{16,20},{20,24},{24,28},{1,5},{5,9},{9,... | collective-permute-start | bytes 92 | tf_op jit(solution)/shard_map/ppermute | solution.py:24
  16.7 7.3 %copy-start.14 = (bf16[3,256,128]{2,1,0:T(8,128)(2,1)S(1)}, bf16[3,256,128]{2,1,0:T(8,128)(2,1)}, u32[]{:S(2)}) copy-start(bf16[3,256,128]{2,1,0:T(8,128)(2,1)} %param.10) | copy-start | bytes 589828
  17.7 49.0 %copy-start.7 = (bf16[2048,256]{1,0:T(8,128)(2,1)}, bf16[2048,256]{1,0:T(8,128)(2,1)S(1)}, u32[]{:S(2)}) copy-start(bf16[2048,256]{1,0:T(8,128)(2,1)S(1)} %get-tuple-element.38) | copy-start | bytes 3145732
  17.8 50.0 %copy-start.23 = (f32[2048,256]{1,0:T(8,128)}, f32[2048,256]{1,0:T(8,128)S(1)}, u32[]{:S(2)}) copy-start(f32[2048,256]{1,0:T(8,128)S(1)} %get-tuple-element.39) | copy-start | bytes 6291460
  17.8 48.6 %collective-permute-start.2 = (bf16[2048,256]{1,0:T(8,128)(2,1)S(1)}, bf16[2048,256]{1,0:T(8,128)(2,1)S(1)}, u32[]{:S(2)}, u32[]{:S(2)}) collective-permute-start(bf16[2048,256]{1,0:T(8,128)(2,1)S(1)} %get-tuple-element.38), channel_id=1, source_target_pairs={{0,4},{4,8},{8,12},{12,16},{16,20},{20,24},{24,28},{1,5},{5,9},{9,... | collective-permute-start | bytes 3145736 | tf_op jit(solution)/shard_map/ppermute | solution.py:13
  22.7 44.1 %collective-permute-start.3 = (bf16[2048,256]{1,0:T(8,128)(2,1)S(1)}, bf16[2048,256]{1,0:T(8,128)(2,1)S(1)}, u32[]{:S(2)}, u32[]{:S(2)}) collective-permute-start(bf16[2048,256]{1,0:T(8,128)(2,1)S(1)} %get-tuple-element.38), channel_id=1, source_target_pairs={{4,0},{8,4},{12,8},{16,12},{20,16},{24,20},{28,24},{5,1},{9,5},{13... | collective-permute-start | bytes 3145736 | tf_op jit(solution)/shard_map/ppermute | solution.py:13
  66.3 1.0 copy-start.3
  66.8 1.0 copy-start.18
  66.8 1.0 copy-start.5
  67.8 2.3 copy-start.1
  67.8 9.9 %copy-start.17 = (bf16[1,192,128]{2,1,0:T(8,128)(2,1)S(1)}, bf16[1,192,128]{2,1,0:T(8,128)(2,1)}, u32[]{:S(2)}) copy-start(bf16[1,192,128]{2,1,0:T(8,128)(2,1)} %param.15) | copy-start | bytes 147460
  67.8 10.8 %copy-start.13 = (bf16[3,256,128]{2,1,0:T(8,128)(2,1)S(1)}, bf16[3,256,128]{2,1,0:T(8,128)(2,1)}, u32[]{:S(2)}) copy-start(bf16[3,256,128]{2,1,0:T(8,128)(2,1)} %param.12) | copy-start | bytes 589828
  70.1 29.4 %collective-permute-start.4 = (bf16[2048,256]{1,0:T(8,128)(2,1)S(1)}, bf16[2048,256]{1,0:T(8,128)(2,1)S(1)}, u32[]{:S(2)}, u32[]{:S(2)}) collective-permute-start(bf16[2048,256]{1,0:T(8,128)(2,1)S(1)} %get-tuple-element.40), channel_id=1, source_target_pairs={{0,8},{4,12},{8,16},{12,20},{16,24},{20,28},{1,9},{5,13},{9,17},{1... | collective-permute-start | bytes 3145736 | tf_op jit(solution)/shard_map/ppermute | solution.py:13
  76.4 27.5 %collective-permute-start.5 = (bf16[2048,256]{1,0:T(8,128)(2,1)S(1)}, bf16[2048,256]{1,0:T(8,128)(2,1)S(1)}, u32[]{:S(2)}, u32[]{:S(2)}) collective-permute-start(bf16[2048,256]{1,0:T(8,128)(2,1)S(1)} %get-tuple-element.40), channel_id=1, source_target_pairs={{8,0},{12,4},{16,8},{20,12},{24,16},{28,20},{9,1},{13,5},{17,9},{2... | collective-permute-start | bytes 3145736 | tf_op jit(solution)/shard_map/ppermute | solution.py:13
  78.6 158.8 %all-reduce.7.cloned.1.call-start = ((), (), s32[]{:S(2)}) async-start(), calls=%async_computation.3 | async-start | bytes 2490368 | tf_op jit(solution)/shard_map/psum | solution.py:53
  100.0 6.2 %copy-start.11 = (bf16[2048,256]{1,0:T(8,128)(2,1)S(1)}, bf16[2048,256]{1,0:T(8,128)(2,1)}, u32[]{:S(2)}) copy-start(bf16[2048,256]{1,0:T(8,128)(2,1)} %get-tuple-element.41) | copy-start | bytes 3145732
  100.0 6.2 %copy-start.19 = (bf16[128,256]{1,0:T(8,128)(2,1)S(1)}, bf16[128,256]{1,0:T(8,128)(2,1)}, u32[]{:S(2)}) copy-start(bf16[128,256]{1,0:T(8,128)(2,1)} %param.13) | copy-start | bytes 196612
  105.3 0.8 copy-start.9
  141.4 3.0 copy-start.10
  141.4 3.0 copy-start.20
  145.4 40.8 %collective-permute-start.6 = (bf16[2048,128]{1,0:T(8,128)(2,1)S(1)}, bf16[2048,128]{1,0:T(8,128)(2,1)S(1)}, u32[]{:S(2)}, u32[]{:S(2)}) collective-permute-start(bf16[2048,128]{1,0:T(8,128)(2,1)S(1)} %fusion.7), channel_id=1, source_target_pairs={{8,0},{12,4},{16,8},{20,12},{24,16},{28,20},{9,1},{13,5},{17,9},{2... | collective-permute-start | bytes 1572872 | tf_op jit(solution)/shard_map/ppermute | solution.py:13
  146.7 39.9 %collective-permute-start.7 = (bf16[2048,128]{1,0:T(8,128)(2,1)S(1)}, bf16[2048,128]{1,0:T(8,128)(2,1)S(1)}, u32[]{:S(2)}, u32[]{:S(2)}) collective-permute-start(bf16[2048,128]{1,0:T(8,128)(2,1)S(1)} %fusion.7), channel_id=1, source_target_pairs={{0,8},{4,12},{8,16},{12,20},{16,24},{20,28},{1,9},{5,13},{9,17},{1... | collective-permute-start | bytes 1572872 | tf_op jit(solution)/shard_map/ppermute | solution.py:13
  186.2 1.2 copy-start.12
  186.6 1.9 copy-start.2
  188.5 1.2 copy-start.8
  188.6 8.4 %copy-start.6 = (bf16[2048,256]{1,0:T(8,128)(2,1)S(1)}, bf16[2048,256]{1,0:T(8,128)(2,1)}, u32[]{:S(2)}) copy-start(bf16[2048,256]{1,0:T(8,128)(2,1)} %copy-done.5) | copy-start | bytes 3145732
  189.8 7.6 %copy-start.4 = (bf16[2048,256]{1,0:T(8,128)(2,1)S(1)}, bf16[2048,256]{1,0:T(8,128)(2,1)}, u32[]{:S(2)}) copy-start(bf16[2048,256]{1,0:T(8,128)(2,1)} %copy-done.3) | copy-start | bytes 3145732
  190.2 11.1 %collective-permute-start.8 = (bf16[2048,128]{1,0:T(8,128)(2,1)S(1)}, bf16[2048,128]{1,0:T(8,128)(2,1)S(1)}, u32[]{:S(2)}, u32[]{:S(2)}) collective-permute-start(bf16[2048,128]{1,0:T(8,128)(2,1)S(1)} %fusion.8), channel_id=1, source_target_pairs={{4,0},{8,4},{12,8},{16,12},{20,16},{24,20},{28,24},{5,1},{9,5},{13... | collective-permute-start | bytes 1572872 | tf_op jit(solution)/shard_map/ppermute | solution.py:13
  191.6 45.8 %collective-permute-start.9 = (bf16[2048,128]{1,0:T(8,128)(2,1)S(1)}, bf16[2048,128]{1,0:T(8,128)(2,1)}, u32[]{:S(2)}, u32[]{:S(2)}) collective-permute-start(bf16[2048,128]{1,0:T(8,128)(2,1)S(1)} %fusion.8), channel_id=1, source_target_pairs={{0,4},{4,8},{8,12},{12,16},{16,20},{20,24},{24,28},{1,5},{5,9},{9,... | collective-permute-start | bytes 1572872 | tf_op jit(solution)/shard_map/ppermute | solution.py:13
  198.7 1.1 copy-start.15
  199.8 120.9 %all-reduce.5.cloned.1.call-start = ((), (), s32[]{:S(2)}) async-start(), calls=%async_computation.2 | async-start | bytes 2097152 | tf_op jit(solution)/shard_map/psum | solution.py:53
  200.3 37.1 %copy-start.22 = (bf16[60,256]{1,0:T(8,128)(2,1)S(1)}, bf16[60,256]{1,0:T(8,128)(2,1)}, u32[]{:S(2)}) copy-start(bf16[60,256]{1,0:T(8,128)(2,1)} %param.9) | copy-start | bytes 92164
  242.0 10.8 %copy-start.16 = (f32[192,256]{1,0:T(8,128)S(1)}, f32[192,256]{1,0:T(8,128)}, u32[]{:S(2)}) copy-start(f32[192,256]{1,0:T(8,128)} %get-tuple-element.15) | copy-start | bytes 589828
  242.0 5.6 %collective-permute-start.10 = (bf16[7,60]{0,1:T(8,128)(2,1)S(1)}, bf16[7,60]{0,1:T(8,128)(2,1)S(1)}, u32[]{:S(2)}, u32[]{:S(2)}) collective-permute-start(bf16[7,60]{0,1:T(8,128)(2,1)S(1)} %get-tuple-element.17), channel_id=1, source_target_pairs={{0,4},{4,8},{8,12},{12,16},{16,20},{20,24},{24,28},{1,5},{5,9},{9,... | collective-permute-start | bytes 2528 | tf_op jit(solution)/shard_map/ppermute | solution.py:24
  245.5 5.9 %collective-permute-start.11 = (bf16[7,60]{0,1:T(8,128)(2,1)S(1)}, bf16[7,60]{0,1:T(8,128)(2,1)S(1)}, u32[]{:S(2)}, u32[]{:S(2)}) collective-permute-start(bf16[7,60]{0,1:T(8,128)(2,1)S(1)} %get-tuple-element.16), channel_id=1, source_target_pairs={{4,0},{8,4},{12,8},{16,12},{20,16},{24,20},{28,24},{5,1},{9,5},{13... | collective-permute-start | bytes 2528 | tf_op jit(solution)/shard_map/ppermute | solution.py:26
Sparse Core Ops, SparseCore 0:
  78.7 62.6 reduce-scatter.1
  199.9 37.3 all-reduce.6
  241.6 79.0 all-reduce.4
